TPU v7x, 32 devices: a whole 2x2x4 slice. The times are simulated.
32 devices in a mesh: section: 4 (over x, core), seq: 8 (over z, y).
Axes of the slice: x: 2, y: 2, z: 4, core: 2. Of those that a mesh axis runs over, the one named last changes fastest.
Arguments:
- hidden: bfloat16 [2, 1024, 2688], P(None, 'seq'), may hold values from -6 to 6
- lengths: int32 [2], replicated, may hold values from 512 to 1024, as said below
- reward_pos: int32 [2], replicated, may hold values from 384 to 1023, as said below
- in_gain: bfloat16 [2688], P('seq'), may hold values from 0.099609375 to 1.8984375
- w_query: bfloat16 [2688, 2048], P('seq', 'section'), may hold values from -0.077151675 to 0.077151675
- w_key: bfloat16 [2688, 1024], P('seq', 'section'), may hold values from -0.077151675 to 0.077151675
- w_value: bfloat16 [2688, 1024], P('seq', 'section'), may hold values from -0.125 to 0.125
- query_gain: float32 [128], replicated, may hold values from 0.6 to 7
- key_gain: float32 [128], replicated, may hold values from 0.6 to 7
- w_out: bfloat16 [2048, 2688], P('section', 'seq'), may hold values from -0.125 to 0.125
- post_gain: bfloat16 [2688], P('seq'), may hold values from 0.099609375 to 1.8984375
- final_gain: bfloat16 [2688], P('seq'), may hold values from 0.099609375 to 1.8984375
- value_head: bfloat16 [2688], P('seq'), may hold values from -0.125 to 0.125
Outputs:
- token_values: float32 [2, 1024], P(None, 'seq')
- reward: float32 [2], replicated
Inputs may be any that keep to these rules, and one draw needn't show every extreme that they name: `lengths`: in every draw at least one micro-batch has all 1024 tokens valid. reward_pos[m] lies among the last 128 valid tokens of micro-batch m.
All inputs are finite; a program needn't handle non-finite values.
Results may differ from a plain program's by a relative error of at most 0.01.
Values may be sent and summed in bfloat16 or wider, within the bound.
A program may use at most 64 MiB of HBM per device.

v0:
```python
import jax
import jax.numpy as jnp
from jax import lax
from jax.sharding import PartitionSpec as P

HD = 128
GROUP = 2
WINDOW = 1024
norm_eps = 1e-06
query_scale = 168.0 ** (-0.5)
rope_base = 10000.0


def passed_along(array, axis, by):
    devices = lax.axis_size(axis)
    pairs = [(i, i + by) for i in range(devices) if 0 <= i + by < devices]
    return lax.ppermute(array, axis, pairs)


def rms_scale(values, gain_vec):
    return (
        values * lax.rsqrt(jnp.mean(values * values, axis=-1, keepdims=True) + norm_eps) * gain_vec
    )


def rotate_pairs(head_rows, positions):
    half_width = head_rows.shape[-1] // 2
    frequency = rope_base ** (
        -jnp.arange(half_width, dtype=jnp.float32) * 2.0 / head_rows.shape[-1]
    )
    angles = positions.astype(jnp.float32)[:, None] * frequency[None, :]
    target = (angles.shape[0],) + (1,) * (head_rows.ndim - 2) + (half_width,)
    cosine = jnp.cos(angles).reshape(target)
    sine_part = jnp.sin(angles).reshape(target)
    front_half = head_rows[..., :half_width]
    back_half = head_rows[..., half_width:]
    return jnp.concatenate(
        [front_half * cosine - back_half * sine_part, back_half * cosine + front_half * sine_part],
        axis=-1,
    )


def window_blocks(packed, tok_dev):
    block_count = WINDOW // tok_dev + 1
    blocks_held = [packed]
    for offset in range(1, block_count):
        blocks_held.append(passed_along(packed, "seq", offset))
    return jnp.concatenate(blocks_held[::-1], axis=1)


def window_attention(queries, keys_all, values_all, query_pos, key_pos):
    scores = jnp.einsum("qhgd,khd->hgqk", queries, keys_all, preferred_element_type=jnp.float32)
    allowed = (
        (key_pos[None, :] <= query_pos[:, None])
        & (key_pos[None, :] > query_pos[:, None] - WINDOW)
        & (key_pos[None, :] >= 0)
    )
    scores = jnp.where(allowed[None, None], scores, -1e30)
    row_top = jnp.max(scores, axis=-1, keepdims=True)
    exponent = jnp.exp(scores - row_top)
    attn_weights = (exponent / jnp.sum(exponent, axis=-1, keepdims=True)).astype(jnp.bfloat16)
    mixed_heads = jnp.einsum(
        "hgqk,khd->qhgd", attn_weights, values_all, preferred_element_type=jnp.float32
    )
    return mixed_heads.astype(jnp.bfloat16)


def local(
    hidden,
    lengths,
    reward_pos,
    in_gain,
    w_query,
    w_key,
    w_value,
    query_gain,
    key_gain,
    w_out,
    post_gain,
    final_gain,
    value_head,
):
    micro_count, tok_dev, width = hidden.shape
    row_count = micro_count * tok_dev
    qwidth = w_query.shape[1]
    kwidth = w_key.shape[1]
    heads_here = kwidth // HD
    widened = hidden.reshape(row_count, width).astype(jnp.float32)
    inverse = lax.rsqrt(jnp.mean(widened * widened, axis=-1, keepdims=True) + norm_eps)
    seq_pos = lax.axis_index("seq") * tok_dev + jnp.arange(tok_dev, dtype=jnp.int32)
    positions = jnp.tile(seq_pos, micro_count)
    gain_piece = lax.all_gather(in_gain, "seq", axis=0, tiled=True)
    query_piece = lax.all_gather(w_query, "seq", axis=0, tiled=True)
    key_piece = lax.all_gather(w_key, "seq", axis=0, tiled=True)
    value_piece = lax.all_gather(w_value, "seq", axis=0, tiled=True)
    post_piece = lax.all_gather(post_gain, "seq", axis=0, tiled=True)
    final_piece = lax.all_gather(final_gain, "seq", axis=0, tiled=True)
    head_piece = lax.all_gather(value_head, "seq", axis=0, tiled=True)
    normed = (widened * inverse * gain_piece.astype(jnp.float32)).astype(jnp.bfloat16)
    query_acc = jnp.dot(normed, query_piece, preferred_element_type=jnp.float32)
    key_acc = jnp.dot(normed, key_piece, preferred_element_type=jnp.float32)
    value_acc = jnp.dot(normed, value_piece, preferred_element_type=jnp.float32)
    post_full = post_piece.astype(jnp.float32)
    final_full = final_piece.astype(jnp.float32)
    head_full = head_piece.astype(jnp.float32)
    folded = (query_acc, key_acc, value_acc, post_full, final_full, head_full)
    queries = folded[0].reshape(row_count, heads_here, GROUP, HD)
    queries = (rotate_pairs(rms_scale(queries, query_gain), positions) * query_scale).astype(
        jnp.bfloat16
    )
    keys_new = folded[1].reshape(row_count, heads_here, HD)
    keys_new = (
        rotate_pairs(rms_scale(keys_new, key_gain), positions)
        .astype(jnp.bfloat16)
        .reshape(row_count, kwidth)
    )
    vals_new = folded[2].astype(jnp.bfloat16)
    packed = jnp.concatenate([keys_new, vals_new], axis=1).reshape(micro_count, tok_dev, 2 * kwidth)
    window_rows = window_blocks(packed, tok_dev)
    key_pos = seq_pos[0] - WINDOW + jnp.arange(WINDOW + tok_dev, dtype=jnp.int32)
    mixed_list = []
    for micro_id in range(micro_count):
        block_queries = queries[micro_id * tok_dev : (micro_id + 1) * tok_dev]
        keys_all = window_rows[micro_id, :, :kwidth].reshape(-1, heads_here, HD)
        values_all = window_rows[micro_id, :, kwidth:].reshape(-1, heads_here, HD)
        mixed_list.append(
            window_attention(block_queries, keys_all, values_all, seq_pos, key_pos).reshape(
                tok_dev, qwidth
            )
        )
    mixed_all = jnp.concatenate(mixed_list, axis=0)
    branch = jnp.dot(
        mixed_all,
        lax.all_gather(w_out, "seq", axis=1, tiled=True),
        preferred_element_type=jnp.float32,
    )
    post_full, final_full, head_full = (folded[3], folded[4], folded[5])
    share_width = width // lax.axis_size("section")
    offset = lax.axis_index("section") * share_width
    share = lax.psum_scatter(branch, "section", scatter_dimension=1, tiled=True)
    branch_sq = lax.psum(jnp.sum(share * share, axis=1), "section")
    share_scale = lax.rsqrt(branch_sq / width + norm_eps)[:, None]
    post_share = lax.dynamic_slice_in_dim(post_full, offset, share_width, 0)
    updated = (
        lax.dynamic_slice_in_dim(widened, offset, share_width, 1) + share * share_scale * post_share
    ).astype(jnp.bfloat16)
    updated_wide = updated.astype(jnp.float32)
    residual_sq = lax.psum(jnp.sum(updated_wide * updated_wide, axis=1), "section")
    final_share = lax.dynamic_slice_in_dim(final_full, offset, share_width, 0)
    last_rows = (
        updated_wide * lax.rsqrt(residual_sq / width + norm_eps)[:, None] * final_share
    ).astype(jnp.bfloat16)
    head_share = lax.dynamic_slice_in_dim(head_full, offset, share_width, 0).astype(jnp.bfloat16)
    raw_values = lax.psum(
        jnp.dot(last_rows, head_share, preferred_element_type=jnp.float32), "section"
    )
    raw_values = raw_values.reshape(micro_count, tok_dev)
    token_values = jnp.where(seq_pos[None, :] < lengths[:, None], raw_values, 0.0)
    partial_value = jnp.sum(
        jnp.where(seq_pos[None, :] == reward_pos[:, None], token_values, 0.0), axis=1
    )
    reward = lax.psum(partial_value, "seq")
    return (token_values, reward)


def solution(mesh):
    placed = (
        P(None, "seq", None),
        P(),
        P(),
        P("seq"),
        P("seq", "section"),
        P("seq", "section"),
        P("seq", "section"),
        P(),
        P(),
        P("section", "seq"),
        P("seq"),
        P("seq"),
        P("seq"),
    )
    return jax.shard_map(
        local, mesh=mesh, in_specs=placed, out_specs=(P(None, "seq"), P()), check_vma=False
    )
```

profile of v0, /device:TPU:0, one launch (start us, length us, event | category | flops | bytes accessed | tf_op | source)
XLA Modules:
  0.0 331.5 jit_solution(10913897586998984354)
XLA Ops:
  15.5 39.5 %all-reduce.4 = (bf16[2688]{0:T(1024)(128)(2,1)S(1)}, bf16[2688]{0:T(1024)(128)(2,1)S(1)}, bf16[2688]{0:T(1024)(128)(2,1)S(1)}, bf16[2688]{0:T(1024)(128)(2,1)S(1)}) all-reduce(bf16[2688]{0:T(1024)(128)(2,1)S(1)} %dynamic-update-slice.3, bf16[2688]{0:T(1024)(128)(2,1)S(1)} %dynamic-update-slice, ...), channel_id=1, replica_groups=mesh['section'=4,'seq'=8] {'seq'}, use_global_device_ids=true, to_apply=%add.3 | all-reduce | flops 10752 | bytes 43008
  58.4 2.9 multiply_convert_fusion.1
  61.7 2.6 copy.24
  66.9 31.5 %all-gather.7.cloned.1.call-done = bf16[2688,256]{1,0:T(8,128)(2,1)} async-done(((bf16[336,256]{1,0:T(8,128)(2,1)}), bf16[2688,256]{1,0:T(8,128)(2,1)}) %all-gather.7.cloned.1.call-update) | async-done | bytes 1376272 | tf_op jit(solution)/shard_map/all_gather | solution.py:95
  101.6 4.0 %collective-permute-start.1 = (bf16[2,128,512]{1,2,0:T(8,128)(2,1)S(1)}, bf16[2,128,512]{1,2,0:T(8,128)(2,1)S(1)}, u32[]{:S(2)}, u32[]{:S(2)}) collective-permute-start(bf16[2,128,512]{1,2,0:T(8,128)(2,1)S(1)} %pad_maximum_fusion), channel_id=1, source_target_pairs={{0,7},{8,15},{16,23},{24,31}} | collective-permute-start | bytes 786440 | tf_op jit(solution)/shard_map/ppermute | solution.py:17
  111.0 2.4 collective-permute-start.5
  113.6 2.9 collective-permute-done.1
  117.8 9.9 %collective-permute-done.2 = bf16[2,128,512]{1,2,0:T(8,128)(2,1)S(1)} collective-permute-done((bf16[2,128,512]{1,2,0:T(8,128)(2,1)S(1)}, bf16[2,128,512]{1,2,0:T(8,128)(2,1)S(1)}, u32[]{:S(2)}, u32[]{:S(2)}) %collective-permute-start.2) | collective-permute-done | bytes 262176 | tf_op jit(solution)/shard_map/ppermute | solution.py:17
  129.2 5.3 %collective-permute-done.3 = bf16[2,128,512]{1,2,0:T(8,128)(2,1)S(1)} collective-permute-done((bf16[2,128,512]{1,2,0:T(8,128)(2,1)S(1)}, bf16[2,128,512]{1,2,0:T(8,128)(2,1)S(1)}, u32[]{:S(2)}, u32[]{:S(2)}) %collective-permute-start.3) | collective-permute-done | bytes 262176 | tf_op jit(solution)/shard_map/ppermute | solution.py:17
  134.6 5.6 %collective-permute-done.4 = bf16[2,128,512]{1,2,0:T(8,128)(2,1)S(1)} collective-permute-done((bf16[2,128,512]{1,2,0:T(8,128)(2,1)S(1)}, bf16[2,128,512]{1,2,0:T(8,128)(2,1)S(1)}, u32[]{:S(2)}, u32[]{:S(2)}) %collective-permute-start.4) | collective-permute-done | bytes 262176 | tf_op jit(solution)/shard_map/ppermute | solution.py:17
  140.3 5.6 %collective-permute-done.5 = bf16[2,128,512]{1,2,0:T(8,128)(2,1)S(1)} collective-permute-done((bf16[2,128,512]{1,2,0:T(8,128)(2,1)S(1)}, bf16[2,128,512]{1,2,0:T(8,128)(2,1)S(1)}, u32[]{:S(2)}, u32[]{:S(2)}) %collective-permute-start.5) | collective-permute-done | bytes 262176 | tf_op jit(solution)/shard_map/ppermute | solution.py:17
  145.9 3.4 %collective-permute-done.6 = bf16[2,128,512]{1,2,0:T(8,128)(2,1)S(1)} collective-permute-done((bf16[2,128,512]{1,2,0:T(8,128)(2,1)S(1)}, bf16[2,128,512]{1,2,0:T(8,128)(2,1)S(1)}, u32[]{:S(2)}, u32[]{:S(2)}) %collective-permute-start.6) | collective-permute-done | bytes 262176 | tf_op jit(solution)/shard_map/ppermute | solution.py:17
  150.8 27.7 %all-gather.9.cloned.1.call-done = bf16[2688,512]{1,0:T(8,128)(2,1)} async-done(((bf16[336,512]{1,0:T(8,128)(2,1)}), bf16[2688,512]{1,0:T(8,128)(2,1)}) %all-gather.9.cloned.1.call-update) | async-done | bytes 2752528 | tf_op jit(solution)/shard_map/all_gather | solution.py:93
  178.5 4.5 %copy.27 = bf16[512,2688]{1,0:T(8,128)(2,1)} copy(bf16[512,2688]{0,1:T(8,128)(2,1)} %bitcast.94) | data formatting | bytes 5505024 | tf_op jit(solution)/shard_map/dot_general | solution.py:100
  183.0 3.2 multiply_reduce_fusion.2
  191.1 3.2 fusion.14
  194.3 3.1 fusion.13
  197.3 46.1 %all-gather.11.cloned.1.call-done = bf16[512,2688]{0,1:T(8,128)(2,1)} async-done(((bf16[512,336]{0,1:T(8,128)(2,1)}), bf16[512,2688]{0,1:T(8,128)(2,1)}) %all-gather.11.cloned.1.call-update) | async-done | bytes 2752528 | tf_op jit(solution)/shard_map/all_gather | solution.py:134
  243.4 4.3 %fusion.24 = f32[256,2688]{0,1:T(8,128)} fusion(bf16[512,2688]{0,1:T(8,128)(2,1)} %all-gather.11.cloned.1.call-done, bf16[128,512]{0,1:T(8,128)(2,1)} %bitcast.108, bf16[128,512]{0,1:T(8,128)(2,1)} %bitcast.107), kind=kOutput, calls=%fused_computation.39 | convolution fusion | flops 705167360 | bytes 5767168 | tf_op jit(solution)/shard_map/dot_general | solution.py:132
  248.0 33.8 %reduce-scatter.2.cloned.1.call-done = f32[256,672]{0,1:T(8,128)} async-done(((f32[256,2688]{0,1:T(8,128)}), f32[256,672]{0,1:T(8,128)}) %reduce-scatter.2.cloned.1.call-update) | async-done | bytes 688144 | tf_op jit(solution)/shard_map/reduce_scatter | solution.py:140
  283.0 5.8 %psum.28 = f32[256]{0:T(256)S(1)} all-reduce(f32[256]{0:T(256)S(1)} %multiply_reduce_fusion.1), channel_id=1, replica_groups=mesh['section'=4,'seq'=8] {'section'}, use_global_device_ids=true, to_apply=%region_9.10 | all-reduce | flops 256 | bytes 2048 | tf_op jit(solution)/shard_map/psum | solution.py:141
  290.1 5.7 %psum.29 = f32[256]{0:T(256)S(1)} all-reduce(f32[256]{0:T(256)S(1)} %get-tuple-element.8), channel_id=1, replica_groups=mesh['section'=4,'seq'=8] {'section'}, use_global_device_ids=true, to_apply=%region_11.12 | all-reduce | flops 256 | bytes 2048 | tf_op jit(solution)/shard_map/psum | solution.py:148
  296.0 6.3 %psum.30 = f32[2,128]{1,0:T(2,128)S(1)} all-reduce(f32[2,128]{1,0:T(2,128)S(1)} %bitcast.110), channel_id=1, replica_groups=mesh['section'=4,'seq'=8] {'section'}, use_global_device_ids=true, to_apply=%region_12.13 | all-reduce | flops 256 | bytes 2048 | tf_op jit(solution)/shard_map/psum | solution.py:154
  303.1 21.9 %psum.31 = f32[2]{0:T(128)} all-reduce(f32[2]{0:T(128)S(1)} %get-tuple-element.6), channel_id=1, replica_groups=mesh['section'=4,'seq'=8] {'seq'}, use_global_device_ids=true, to_apply=%region_14.15 | all-reduce | flops 2 | bytes 16 | tf_op jit(solution)/shard_map/psum | solution.py:162
  (86 shorter events, 35.6 us)
Async XLA Ops:
  7.2 54.5 %all-gather.5.cloned.1.call-start = ((), (), s32[]{:S(2)}) async-start(), calls=%async_computation.1 | async-start | bytes 1548288 | tf_op jit(solution)/shard_map/all_gather | solution.py:94
  7.9 90.5 %all-gather.7.cloned.1.call-start = ((), (), s32[]{:S(2)}) async-start(), calls=%async_computation.2 | async-start | bytes 1548288 | tf_op jit(solution)/shard_map/all_gather | solution.py:95
  8.6 169.8 %all-gather.9.cloned.1.call-start = ((), (), s32[]{:S(2)}) async-start(), calls=%async_computation.3 | async-start | bytes 3096576 | tf_op jit(solution)/shard_map/all_gather | solution.py:93
  9.4 234.0 %all-gather.11.cloned.1.call-start = ((), (), s32[]{:S(2)}) async-start(), calls=%async_computation.4 | async-start | bytes 3096576 | tf_op jit(solution)/shard_map/all_gather | solution.py:134
  10.0 271.8 %reduce-scatter.2.cloned.1.call-start = ((), (), s32[]{:S(2)}) async-start(), calls=%async_computation.5 | async-start | bytes 3440640 | tf_op jit(solution)/shard_map/reduce_scatter | solution.py:140
  61.7 5.0 %copy-start.1 = (f32[128]{0:T(128)S(1)}, f32[128]{0:T(128)}, u32[]{:S(2)}) copy-start(f32[128]{0:T(128)} %param.21) | copy-start | bytes 1540
  100.9 10.1 %collective-permute-start = (bf16[2,128,512]{1,2,0:T(8,128)(2,1)S(1)}, bf16[2,128,512]{1,2,0:T(8,128)(2,1)S(1)}, u32[]{:S(2)}, u32[]{:S(2)}) collective-permute-start(bf16[2,128,512]{1,2,0:T(8,128)(2,1)S(1)} %pad_maximum_fusion), channel_id=1, source_target_pairs={} | collective-permute-start | bytes 786440 | tf_op jit(solution)/shard_map/ppermute | solution.py:17
  101.6 14.9 %collective-permute-start.1 = (bf16[2,128,512]{1,2,0:T(8,128)(2,1)S(1)}, bf16[2,128,512]{1,2,0:T(8,128)(2,1)S(1)}, u32[]{:S(2)}, u32[]{:S(2)}) collective-permute-start(bf16[2,128,512]{1,2,0:T(8,128)(2,1)S(1)} %pad_maximum_fusion), channel_id=1, source_target_pairs={{0,7},{8,15},{16,23},{24,31}} | collective-permute-start | bytes 786440 | tf_op jit(solution)/shard_map/ppermute | solution.py:17
  105.6 22.1 %collective-permute-start.2 = (bf16[2,128,512]{1,2,0:T(8,128)(2,1)S(1)}, bf16[2,128,512]{1,2,0:T(8,128)(2,1)S(1)}, u32[]{:S(2)}, u32[]{:S(2)}) collective-permute-start(bf16[2,128,512]{1,2,0:T(8,128)(2,1)S(1)} %pad_maximum_fusion), channel_id=1, source_target_pairs={{0,6},{1,7},{8,14},{9,15},{16,22},{17,23},{24,30},{25,31}} | collective-permute-start | bytes 786440 | tf_op jit(solution)/shard_map/ppermute | solution.py:17
  108.4 26.2 %collective-permute-start.3 = (bf16[2,128,512]{1,2,0:T(8,128)(2,1)S(1)}, bf16[2,128,512]{1,2,0:T(8,128)(2,1)S(1)}, u32[]{:S(2)}, u32[]{:S(2)}) collective-permute-start(bf16[2,128,512]{1,2,0:T(8,128)(2,1)S(1)} %pad_maximum_fusion), channel_id=1, source_target_pairs={{0,5},{1,6},{2,7},{8,13},{9,14},{10,15},{16,21},{17,22},{18,23},{2... | collective-permute-start | bytes 786440 | tf_op jit(solution)/shard_map/ppermute | solution.py:17
  109.7 30.5 %collective-permute-start.4 = (bf16[2,128,512]{1,2,0:T(8,128)(2,1)S(1)}, bf16[2,128,512]{1,2,0:T(8,128)(2,1)S(1)}, u32[]{:S(2)}, u32[]{:S(2)}) collective-permute-start(bf16[2,128,512]{1,2,0:T(8,128)(2,1)S(1)} %pad_maximum_fusion), channel_id=1, source_target_pairs={{0,4},{1,5},{2,6},{3,7},{8,12},{9,13},{10,14},{11,15},{16,20},{17,... | collective-permute-start | bytes 786440 | tf_op jit(solution)/shard_map/ppermute | solution.py:17
  111.0 34.8 %collective-permute-start.5 = (bf16[2,128,512]{1,2,0:T(8,128)(2,1)S(1)}, bf16[2,128,512]{1,2,0:T(8,128)(2,1)S(1)}, u32[]{:S(2)}, u32[]{:S(2)}) collective-permute-start(bf16[2,128,512]{1,2,0:T(8,128)(2,1)S(1)} %pad_maximum_fusion), channel_id=1, source_target_pairs={{0,3},{1,4},{2,5},{3,6},{4,7},{8,11},{9,12},{10,13},{11,14},{12,15... | collective-permute-start | bytes 786440 | tf_op jit(solution)/shard_map/ppermute | solution.py:17
  116.5 32.9 %collective-permute-start.6 = (bf16[2,128,512]{1,2,0:T(8,128)(2,1)S(1)}, bf16[2,128,512]{1,2,0:T(8,128)(2,1)S(1)}, u32[]{:S(2)}, u32[]{:S(2)}) collective-permute-start(bf16[2,128,512]{1,2,0:T(8,128)(2,1)S(1)} %pad_maximum_fusion), channel_id=1, source_target_pairs={{0,2},{1,3},{2,4},{3,5},{4,6},{5,7},{8,10},{9,11},{10,12},{11,13},... | collective-permute-start | bytes 786440 | tf_op jit(solution)/shard_map/ppermute | solution.py:17
  127.7 21.7 %collective-permute-start.7 = (bf16[2,128,512]{1,2,0:T(8,128)(2,1)S(1)}, bf16[2,128,512]{1,2,0:T(8,128)(2,1)S(1)}, u32[]{:S(2)}, u32[]{:S(2)}) collective-permute-start(bf16[2,128,512]{1,2,0:T(8,128)(2,1)S(1)} %pad_maximum_fusion), channel_id=1, source_target_pairs={{0,1},{1,2},{2,3},{3,4},{4,5},{5,6},{6,7},{8,9},{9,10},{10,11},{11... | collective-permute-start | bytes 786440 | tf_op jit(solution)/shard_map/ppermute | solution.py:17
  183.0 3.2 copy-start.2
  186.4 2.9 copy-start
  247.7 54.6 %copy-start.3 = (s32[2]{0:T(128)S(1)}, s32[2]{0:T(128)}, u32[]{:S(2)}) copy-start(s32[2]{0:T(128)} %param.15) | copy-start | bytes 28
  247.7 54.6 %copy-start.4 = (s32[2]{0:T(128)S(1)}, s32[2]{0:T(128)}, u32[]{:S(2)}) copy-start(s32[2]{0:T(128)} %param.14) | copy-start | bytes 28
Sparse Core Ops, SparseCore 0:
  10.2 45.0 all-gather.4
  57.4 40.9 all-gather.6
  100.6 77.8 all-gather.8
  180.5 62.8 all-gather.10
  247.9 33.8 reduce-scatter.1
where the time goes:
time: 332 us; the launch traced here: 331 us
  waiting for transfers between devices  174 us (52%)
  blocking collectives  79.1 us (24%)
  matrix products  22.7 us (7%)
  local copies, waits for them, and re-layouts  15.4 us (5%)
  between operations  14.8 us (4%)
  starting transfers between devices  14 us (4%)
  other arithmetic  11.1 us (3%)
    all_gather x1, waiting for transfers between devices, local(): lax.all_gather(w_out, 'seq', axis=1, tiled=True)  46.1 us
    unnamed x1, blocking collectives  39.5 us
    reduce_scatter x1, waiting for transfers between devices, local(): share = lax.psum_scatter(branch, 'section', scatter_dimension=1, tiled=True)  33.8 us
    ppermute x8, waiting for transfers between devices, passed_along(): return lax.ppermute(array, axis, pairs)  32.7 us
    all_gather x1, waiting for transfers between devices, local(): value_piece = lax.all_gather(w_value, 'seq', axis=0, tiled=True)  31.5 us
    all_gather x1, waiting for transfers between devices, local(): query_piece = lax.all_gather(w_query, 'seq', axis=0, tiled=True)  27.7 us
    psum x1, blocking collectives, local(): reward = lax.psum(partial_value, 'seq')  21.9 us
    ppermute x8, starting transfers between devices, passed_along(): return lax.ppermute(array, axis, pairs)  13.8 us
  transfers between devices with their start and end apart: 13, of which 10 were waited for; matrix products, arithmetic and copies ran while one was open for 12% of the time, Pallas kernels for 0%

commit v1 on v0

--- a/solution.py
+++ b/solution.py
@@ -90,7 +90,13 @@
     seq_pos = lax.axis_index("seq") * tok_dev + jnp.arange(tok_dev, dtype=jnp.int32)
     positions = jnp.tile(seq_pos, micro_count)
     gain_piece = lax.all_gather(in_gain, "seq", axis=0, tiled=True)
-    query_piece = lax.all_gather(w_query, "seq", axis=0, tiled=True)
+    count = lax.axis_size("seq")
+    current, blocks = (w_query, [w_query])
+    for _ in range(count - 1):
+        current = lax.ppermute(current, "seq", [(i_2, (i_2 + 1) % count) for i_2 in range(count)])
+        blocks.insert(0, current)
+    flat = jnp.concatenate(blocks, axis=0)
+    query_piece = jnp.roll(flat, (lax.axis_index("seq") + 1) * w_query.shape[0], axis=0)
     key_piece = lax.all_gather(w_key, "seq", axis=0, tiled=True)
     value_piece = lax.all_gather(w_value, "seq", axis=0, tiled=True)
     post_piece = lax.all_gather(post_gain, "seq", axis=0, tiled=True)

time: 332 us -> 306 us (0.922)
  waiting for transfers between devices: 174 us -> 117 us
  local copies, waits for them, and re-layouts: 15.4 us -> 35.3 us
  starting transfers between devices: 14 us -> 23.1 us
  other arithmetic: 11.1 us -> 14.6 us
    ppermute x0 -> x7, waiting for transfers between devices: none -> 57.1 us  [local(): lax.ppermute(current, 'seq', [(i_2, (i_2 + 1) % count) for i_2 in range(c...]
    all_gather x1, waiting for transfers between devices: 46.1 us -> 0.01 us  [local(): lax.all_gather(w_out, 'seq', axis=1, tiled=True)]
    all_gather x1, waiting for transfers between devices: 31.5 us -> 0.01 us  [local(): value_piece = lax.all_gather(w_value, 'seq', axis=0, tiled=True)]
    all_gather x1 -> x0, waiting for transfers between devices: 27.7 us -> none  [local(): query_piece = lax.all_gather(w_query, 'seq', axis=0, tiled=True)]
    ppermute x8, waiting for transfers between devices: 32.7 us -> 9.54 us  [passed_along(): return lax.ppermute(array, axis, pairs)]
    reduce_scatter x1, waiting for transfers between devices: 33.8 us -> 49 us  [local(): share = lax.psum_scatter(branch, 'section', scatter_dimension=1, tiled=True)]
    unnamed x27 -> x58, local copies, waits for them, and re-layouts: 5.26 us -> 18.2 us
    ppermute x8, starting transfers between devices: 13.8 us -> 19.8 us  [passed_along(): return lax.ppermute(array, axis, pairs)]
  transfers between devices with their start and end apart: 13 -> 19, of which waited for: 10 -> 8; matrix products, arithmetic and copies ran while one was open for 12% -> 21% of each run, Pallas kernels for 0% -> 0%
where the time goes in v1:
time: 306 us; the launch traced here: 305 us
  waiting for transfers between devices  117 us (38%)
  blocking collectives  76.7 us (25%)
  local copies, waits for them, and re-layouts  35.3 us (12%)
  matrix products  23.2 us (8%)
  starting transfers between devices  23.1 us (8%)
  between operations  14.9 us (5%)
  other arithmetic  14.6 us (5%)
    ppermute x7, waiting for transfers between devices, local(): lax.ppermute(current, 'seq', [(i_2, (i_2 + 1) % count) for i_2 in range(c...  57.1 us
    reduce_scatter x1, waiting for transfers between devices, local(): share = lax.psum_scatter(branch, 'section', scatter_dimension=1, tiled=True)  49 us
    unnamed x1, blocking collectives  37.2 us
    psum x1, blocking collectives, local(): reward = lax.psum(partial_value, 'seq')  21.9 us
    ppermute x8, starting transfers between devices, passed_along(): return lax.ppermute(array, axis, pairs)  19.8 us
    unnamed x58, local copies, waits for them, and re-layouts  18.2 us
    ppermute x8, waiting for transfers between devices, passed_along(): return lax.ppermute(array, axis, pairs)  9.54 us
    dot_general x2, local copies, waits for them, and re-layouts, local(): query_acc = jnp.dot(normed, query_piece, preferred_element_type=jnp.float32)  6.72 us
  transfers between devices with their start and end apart: 19, of which 8 were waited for; matrix products, arithmetic and copies ran while one was open for 21% of the time, Pallas kernels for 0%

profile of v1, /device:TPU:0, one launch (start us, length us, event | category | flops | bytes accessed | tf_op | source)
XLA Modules:
  0.0 304.9 jit_solution(17635762349784366831)
XLA Ops:
  8.7 3.0 collective-permute-start.8
  17.2 37.2 %all-reduce.4 = (bf16[2688]{0:T(1024)(128)(2,1)}, bf16[2688]{0:T(1024)(128)(2,1)S(1)}, bf16[2688]{0:T(1024)(128)(2,1)S(1)}, bf16[2688]{0:T(1024)(128)(2,1)S(1)}) all-reduce(bf16[2688]{0:T(1024)(128)(2,1)S(1)} %dynamic-update-slice.3, bf16[2688]{0:T(1024)(128)(2,1)S(1)} %dynamic-update-slice, ...), channel_id=1, replica_groups=mesh['section'=4,'seq'=8] {'seq'}, use_global_device_ids=true, to_apply=%add.3 | all-reduce | flops 10752 | bytes 43008
  56.2 8.2 %collective-permute-done.9 = bf16[336,512]{1,0:T(8,128)(2,1)S(1)} collective-permute-done((bf16[336,512]{1,0:T(8,128)(2,1)S(1)}, bf16[336,512]{1,0:T(8,128)(2,1)S(1)}, u32[]{:S(2)}, u32[]{:S(2)}) %collective-permute-start.9) | collective-permute-done | bytes 344096 | tf_op jit(solution)/shard_map/ppermute | solution.py:96
  66.0 13.1 %collective-permute-done.10 = bf16[336,512]{1,0:T(8,128)(2,1)S(1)} collective-permute-done((bf16[336,512]{1,0:T(8,128)(2,1)S(1)}, bf16[336,512]{1,0:T(8,128)(2,1)S(1)}, u32[]{:S(2)}, u32[]{:S(2)}) %collective-permute-start.10) | collective-permute-done | bytes 344096 | tf_op jit(solution)/shard_map/ppermute | solution.py:96
  79.1 10.0 %collective-permute-done.11 = bf16[336,512]{1,0:T(8,128)(2,1)} collective-permute-done((bf16[336,512]{1,0:T(8,128)(2,1)S(1)}, bf16[336,512]{1,0:T(8,128)(2,1)}, u32[]{:S(2)}, u32[]{:S(2)}) %collective-permute-start.11) | collective-permute-done | bytes 344096 | tf_op jit(solution)/shard_map/ppermute | solution.py:96
  92.9 13.5 %collective-permute-done.12 = bf16[336,512]{1,0:T(8,128)(2,1)} collective-permute-done((bf16[336,512]{1,0:T(8,128)(2,1)}, bf16[336,512]{1,0:T(8,128)(2,1)}, u32[]{:S(2)}, u32[]{:S(2)}) %collective-permute-start.12) | collective-permute-done | bytes 344096 | tf_op jit(solution)/shard_map/ppermute | solution.py:96
  107.9 12.3 %collective-permute-done.13 = bf16[336,512]{1,0:T(8,128)(2,1)} collective-permute-done((bf16[336,512]{1,0:T(8,128)(2,1)}, bf16[336,512]{1,0:T(8,128)(2,1)}, u32[]{:S(2)}, u32[]{:S(2)}) %collective-permute-start.13) | collective-permute-done | bytes 344096 | tf_op jit(solution)/shard_map/ppermute | solution.py:96
  120.2 2.5 copy.24
  122.8 2.4 multiply_reduce_fusion.3
  129.1 3.0 fusion.15
  137.1 7.4 %collective-permute-start.1 = (bf16[2,128,512]{1,2,0:T(8,128)(2,1)}, bf16[2,128,512]{1,2,0:T(8,128)(2,1)}, u32[]{:S(2)}, u32[]{:S(2)}) collective-permute-start(bf16[2,128,512]{1,2,0:T(8,128)(2,1)} %pad_maximum_fusion), channel_id=1, source_target_pairs={{0,7},{8,15},{16,23},{24,31}} | collective-permute-start | bytes 786440 | tf_op jit(solution)/shard_map/ppermute | solution.py:17
  158.8 2.2 dynamic-slice_bitcast_fusion
  161.0 4.5 %copy.27 = bf16[512,2688]{1,0:T(8,128)(2,1)} copy(bf16[512,2688]{0,1:T(8,128)(2,1)} %dynamic-slice_bitcast_fusion) | data formatting | bytes 5505024 | tf_op jit(solution)/shard_map/dot_general | solution.py:106
  165.5 3.2 %multiply_reduce_fusion.2 = (f32[256,2,2]{0,2,1:T(2,128)S(1)}, f32[256,2,2,128]{0,3,2,1:T(8,128)S(1)}) fusion(bf16[256,2688,1,1]{1,0,3,2:T(8,128)(2,1)} %bitcast.97, bf16[2,2,128,2688]{3,2,1,0:T(8,128)(2,1)} %bitcast.95), kind=kOutput, calls=%fused_computation.35 | convolution fusion | flops 704904192 | bytes 4657152 | tf_op jit(solution)/shard_map/dot_general | solution.py:106
  174.4 2.3 collective-permute-start.7
  181.0 8.4 %collective-permute-done.6 = bf16[2,128,512]{1,2,0:T(8,128)(2,1)S(1)} collective-permute-done((bf16[2,128,512]{1,2,0:T(8,128)(2,1)}, bf16[2,128,512]{1,2,0:T(8,128)(2,1)S(1)}, u32[]{:S(2)}, u32[]{:S(2)}) %collective-permute-start.6) | collective-permute-done | bytes 262176 | tf_op jit(solution)/shard_map/ppermute | solution.py:17
  194.7 3.2 %fusion.14 = bf16[2,128,2,128]{3,1,2,0:T(8,128)(2,1)} fusion(bf16[1152,2,128,1]{0,2,3,1:T(8,128)(2,1)} %bitcast.105, f32[2,2,128]{2,1,0:T(2,128)S(1)} %fusion.64, bf16[1152,2,128,1]{0,2,3,1:T(8,128)(2,1)} %bitcast.104, pred[128,1152]{0,1:T(8,128)(4,1)S(1)} %copy-done.8, bf16[256,2,2,128]{0,3,2,1:T(8,128)(2,1)} %fusion.19), kind=kOutput, calls=%fused_computation.22 | convolution fusion | flops 304416384 | bytes 1591296 | tf_op jit(solution)/shard_map/hgqk,khd->qhgd/dot_general | solution.py:62
  197.9 3.0 fusion.13
  200.9 4.3 %fusion.24 = f32[256,2688]{0,1:T(8,128)} fusion(bf16[512,2688]{0,1:T(8,128)(2,1)} %all-gather.8.cloned.1.call-done, bf16[128,512]{0,1:T(8,128)(2,1)} %bitcast.108, bf16[128,512]{0,1:T(8,128)(2,1)} %bitcast.107), kind=kOutput, calls=%fused_computation.40 | convolution fusion | flops 705167360 | bytes 5767168 | tf_op jit(solution)/shard_map/dot_general | solution.py:138
  206.2 49.0 %reduce-scatter.2.cloned.1.call-done = f32[256,672]{0,1:T(8,128)} async-done(((f32[256,2688]{0,1:T(8,128)}), f32[256,672]{0,1:T(8,128)}) %reduce-scatter.2.cloned.1.call-update) | async-done | bytes 688144 | tf_op jit(solution)/shard_map/reduce_scatter | solution.py:146
  256.4 5.8 %psum.28 = f32[256]{0:T(256)S(1)} all-reduce(f32[256]{0:T(256)S(1)} %multiply_reduce_fusion.1), channel_id=1, replica_groups=mesh['section'=4,'seq'=8] {'section'}, use_global_device_ids=true, to_apply=%region_9.10 | all-reduce | flops 256 | bytes 2048 | tf_op jit(solution)/shard_map/psum | solution.py:147
  263.5 5.7 %psum.29 = f32[256]{0:T(256)S(1)} all-reduce(f32[256]{0:T(256)S(1)} %get-tuple-element.8), channel_id=1, replica_groups=mesh['section'=4,'seq'=8] {'section'}, use_global_device_ids=true, to_apply=%region_11.12 | all-reduce | flops 256 | bytes 2048 | tf_op jit(solution)/shard_map/psum | solution.py:154
  269.4 6.3 %psum.30 = f32[2,128]{1,0:T(2,128)S(1)} all-reduce(f32[2,128]{1,0:T(2,128)S(1)} %bitcast.110), channel_id=1, replica_groups=mesh['section'=4,'seq'=8] {'section'}, use_global_device_ids=true, to_apply=%region_12.13 | all-reduce | flops 256 | bytes 2048 | tf_op jit(solution)/shard_map/psum | solution.py:160
  276.5 21.9 %psum.31 = f32[2]{0:T(128)} all-reduce(f32[2]{0:T(128)S(1)} %get-tuple-element.6), channel_id=1, replica_groups=mesh['section'=4,'seq'=8] {'seq'}, use_global_device_ids=true, to_apply=%region_14.15 | all-reduce | flops 2 | bytes 16 | tf_op jit(solution)/shard_map/psum | solution.py:168
  (130 shorter events, 57.6 us)
Async XLA Ops:
  7.2 57.3 %copy-start = (bf16[2,128,2688]{2,1,0:T(8,128)(2,1)S(1)}, bf16[2,128,2688]{2,1,0:T(8,128)(2,1)}, u32[]{:S(2)}) copy-start(bf16[2,128,2688]{2,1,0:T(8,128)(2,1)} %param.13) | copy-start | bytes 4128772
  7.2 113.0 %all-gather.4.cloned.1.call-start = ((), (), s32[]{:S(2)}) async-start(), calls=%async_computation.1 | async-start | bytes 1548288 | tf_op jit(solution)/shard_map/all_gather | solution.py:100
  7.9 121.2 %all-gather.6.cloned.1.call-start = ((), (), s32[]{:S(2)}) async-start(), calls=%async_computation.2 | async-start | bytes 1548288 | tf_op jit(solution)/shard_map/all_gather | solution.py:101
  8.7 192.3 %all-gather.8.cloned.1.call-start = ((), (), s32[]{:S(2)}) async-start(), calls=%async_computation.3 | async-start | bytes 3096576 | tf_op jit(solution)/shard_map/all_gather | solution.py:140
  8.7 45.7 %collective-permute-start.8 = (bf16[336,512]{1,0:T(8,128)(2,1)}, bf16[336,512]{1,0:T(8,128)(2,1)S(1)}, u32[]{:S(2)}, u32[]{:S(2)}) collective-permute-start(bf16[336,512]{1,0:T(8,128)(2,1)} %param.17), channel_id=1, source_target_pairs={{0,1},{1,2},{2,3},{3,4},{4,5},{5,6},{6,7},{7,0},{8,9},{9,10},{10,1... | collective-permute-start | bytes 1032200 | tf_op jit(solution)/shard_map/ppermute | solution.py:96
  11.8 243.4 %reduce-scatter.2.cloned.1.call-start = ((), (), s32[]{:S(2)}) async-start(), calls=%async_computation.4 | async-start | bytes 3440640 | tf_op jit(solution)/shard_map/reduce_scatter | solution.py:146
  54.4 10.0 %collective-permute-start.9 = (bf16[336,512]{1,0:T(8,128)(2,1)S(1)}, bf16[336,512]{1,0:T(8,128)(2,1)S(1)}, u32[]{:S(2)}, u32[]{:S(2)}) collective-permute-start(bf16[336,512]{1,0:T(8,128)(2,1)S(1)} %collective-permute-done.8), channel_id=1, source_target_pairs={{0,1},{1,2},{2,3},{3,4},{4,5},{5,6},{6,7},{7,0},{8,9},{9,10},{10,1... | collective-permute-start | bytes 1032200 | tf_op jit(solution)/shard_map/ppermute | solution.py:96
  64.4 14.7 %collective-permute-start.10 = (bf16[336,512]{1,0:T(8,128)(2,1)S(1)}, bf16[336,512]{1,0:T(8,128)(2,1)S(1)}, u32[]{:S(2)}, u32[]{:S(2)}) collective-permute-start(bf16[336,512]{1,0:T(8,128)(2,1)S(1)} %collective-permute-done.9), channel_id=1, source_target_pairs={{0,1},{1,2},{2,3},{3,4},{4,5},{5,6},{6,7},{7,0},{8,9},{9,10},{10,1... | collective-permute-start | bytes 1032200 | tf_op jit(solution)/shard_map/ppermute | solution.py:96
  79.1 10.1 %collective-permute-start.11 = (bf16[336,512]{1,0:T(8,128)(2,1)S(1)}, bf16[336,512]{1,0:T(8,128)(2,1)}, u32[]{:S(2)}, u32[]{:S(2)}) collective-permute-start(bf16[336,512]{1,0:T(8,128)(2,1)S(1)} %collective-permute-done.10), channel_id=1, source_target_pairs={{0,1},{1,2},{2,3},{3,4},{4,5},{5,6},{6,7},{7,0},{8,9},{9,10},{10,1... | collective-permute-start | bytes 1032200 | tf_op jit(solution)/shard_map/ppermute | solution.py:96
  89.1 17.3 %collective-permute-start.12 = (bf16[336,512]{1,0:T(8,128)(2,1)}, bf16[336,512]{1,0:T(8,128)(2,1)}, u32[]{:S(2)}, u32[]{:S(2)}) collective-permute-start(bf16[336,512]{1,0:T(8,128)(2,1)} %collective-permute-done.11), channel_id=1, source_target_pairs={{0,1},{1,2},{2,3},{3,4},{4,5},{5,6},{6,7},{7,0},{8,9},{9,10},{10,1... | collective-permute-start | bytes 1032200 | tf_op jit(solution)/shard_map/ppermute | solution.py:96
  106.4 13.8 %collective-permute-start.13 = (bf16[336,512]{1,0:T(8,128)(2,1)}, bf16[336,512]{1,0:T(8,128)(2,1)}, u32[]{:S(2)}, u32[]{:S(2)}) collective-permute-start(bf16[336,512]{1,0:T(8,128)(2,1)} %collective-permute-done.12), channel_id=1, source_target_pairs={{0,1},{1,2},{2,3},{3,4},{4,5},{5,6},{6,7},{7,0},{8,9},{9,10},{10,1... | collective-permute-start | bytes 1032200 | tf_op jit(solution)/shard_map/ppermute | solution.py:96
  120.2 28.3 %collective-permute-start.14 = (bf16[336,512]{1,0:T(8,128)(2,1)}, bf16[336,512]{1,0:T(8,128)(2,1)}, u32[]{:S(2)}, u32[]{:S(2)}) collective-permute-start(bf16[336,512]{1,0:T(8,128)(2,1)} %collective-permute-done.13), channel_id=1, source_target_pairs={{0,1},{1,2},{2,3},{3,4},{4,5},{5,6},{6,7},{7,0},{8,9},{9,10},{10,1... | collective-permute-start | bytes 1032200 | tf_op jit(solution)/shard_map/ppermute | solution.py:96
  133.8 20.6 %copy-start.3 = (bf16[336,512]{1,0:T(8,128)(2,1)S(1)}, bf16[336,512]{1,0:T(8,128)(2,1)}, u32[]{:S(2)}) copy-start(bf16[336,512]{1,0:T(8,128)(2,1)} %copy-done.2) | copy-start | bytes 1032196
  135.6 34.1 %collective-permute-start = (bf16[2,128,512]{1,2,0:T(8,128)(2,1)}, bf16[2,128,512]{1,2,0:T(8,128)(2,1)}, u32[]{:S(2)}, u32[]{:S(2)}) collective-permute-start(bf16[2,128,512]{1,2,0:T(8,128)(2,1)} %pad_maximum_fusion), channel_id=1, source_target_pairs={} | collective-permute-start | bytes 786440 | tf_op jit(solution)/shard_map/ppermute | solution.py:17
  137.1 34.9 %collective-permute-start.1 = (bf16[2,128,512]{1,2,0:T(8,128)(2,1)}, bf16[2,128,512]{1,2,0:T(8,128)(2,1)}, u32[]{:S(2)}, u32[]{:S(2)}) collective-permute-start(bf16[2,128,512]{1,2,0:T(8,128)(2,1)} %pad_maximum_fusion), channel_id=1, source_target_pairs={{0,7},{8,15},{16,23},{24,31}} | collective-permute-start | bytes 786440 | tf_op jit(solution)/shard_map/ppermute | solution.py:17
  144.4 29.9 %collective-permute-start.2 = (bf16[2,128,512]{1,2,0:T(8,128)(2,1)}, bf16[2,128,512]{1,2,0:T(8,128)(2,1)}, u32[]{:S(2)}, u32[]{:S(2)}) collective-permute-start(bf16[2,128,512]{1,2,0:T(8,128)(2,1)} %pad_maximum_fusion), channel_id=1, source_target_pairs={{0,6},{1,7},{8,14},{9,15},{16,22},{17,23},{24,30},{25,31}} | collective-permute-start | bytes 786440 | tf_op jit(solution)/shard_map/ppermute | solution.py:17
  146.5 31.2 %collective-permute-start.3 = (bf16[2,128,512]{1,2,0:T(8,128)(2,1)}, bf16[2,128,512]{1,2,0:T(8,128)(2,1)}, u32[]{:S(2)}, u32[]{:S(2)}) collective-permute-start(bf16[2,128,512]{1,2,0:T(8,128)(2,1)} %pad_maximum_fusion), channel_id=1, source_target_pairs={{0,5},{1,6},{2,7},{8,13},{9,14},{10,15},{16,21},{17,22},{18,23},{2... | collective-permute-start | bytes 786440 | tf_op jit(solution)/shard_map/ppermute | solution.py:17
  148.5 30.3 %collective-permute-start.4 = (bf16[2,128,512]{1,2,0:T(8,128)(2,1)}, bf16[2,128,512]{1,2,0:T(8,128)(2,1)}, u32[]{:S(2)}, u32[]{:S(2)}) collective-permute-start(bf16[2,128,512]{1,2,0:T(8,128)(2,1)} %pad_maximum_fusion), channel_id=1, source_target_pairs={{0,4},{1,5},{2,6},{3,7},{8,12},{9,13},{10,14},{11,15},{16,20},{17,... | collective-permute-start | bytes 786440 | tf_op jit(solution)/shard_map/ppermute | solution.py:17
  168.9 20.6 %copy-start.4 = (bf16[2,128,256]{1,2,0:T(8,128)(2,1)S(1)}, bf16[2,128,256]{1,2,0:T(8,128)(2,1)}, u32[]{:S(2)}) copy-start(bf16[2,128,256]{1,2,0:T(8,128)(2,1)} %copy.25) | copy-start | bytes 393220
  169.7 11.2 %collective-permute-start.5 = (bf16[2,128,512]{1,2,0:T(8,128)(2,1)}, bf16[2,128,512]{1,2,0:T(8,128)(2,1)S(1)}, u32[]{:S(2)}, u32[]{:S(2)}) collective-permute-start(bf16[2,128,512]{1,2,0:T(8,128)(2,1)} %pad_maximum_fusion), channel_id=1, source_target_pairs={{0,3},{1,4},{2,5},{3,6},{4,7},{8,11},{9,12},{10,13},{11,14},{12,15... | collective-permute-start | bytes 786440 | tf_op jit(solution)/shard_map/ppermute | solution.py:17
  172.0 17.3 %collective-permute-start.6 = (bf16[2,128,512]{1,2,0:T(8,128)(2,1)}, bf16[2,128,512]{1,2,0:T(8,128)(2,1)S(1)}, u32[]{:S(2)}, u32[]{:S(2)}) collective-permute-start(bf16[2,128,512]{1,2,0:T(8,128)(2,1)} %pad_maximum_fusion), channel_id=1, source_target_pairs={{0,2},{1,3},{2,4},{3,5},{4,6},{5,7},{8,10},{9,11},{10,12},{11,13},... | collective-permute-start | bytes 786440 | tf_op jit(solution)/shard_map/ppermute | solution.py:17
  174.4 15.1 %collective-permute-start.7 = (bf16[2,128,512]{1,2,0:T(8,128)(2,1)}, bf16[2,128,512]{1,2,0:T(8,128)(2,1)S(1)}, u32[]{:S(2)}, u32[]{:S(2)}) collective-permute-start(bf16[2,128,512]{1,2,0:T(8,128)(2,1)} %pad_maximum_fusion), channel_id=1, source_target_pairs={{0,1},{1,2},{2,3},{3,4},{4,5},{5,6},{6,7},{8,9},{9,10},{10,11},{11... | collective-permute-start | bytes 786440 | tf_op jit(solution)/shard_map/ppermute | solution.py:17
  205.2 70.5 %copy-start.11 = (s32[2]{0:T(128)S(1)}, s32[2]{0:T(128)}, u32[]{:S(2)}) copy-start(s32[2]{0:T(128)} %param.15) | copy-start | bytes 28
  205.2 70.5 %copy-start.12 = (s32[2]{0:T(128)S(1)}, s32[2]{0:T(128)}, u32[]{:S(2)}) copy-start(s32[2]{0:T(128)} %param.14) | copy-start | bytes 28
  (8 other events, 65.4 us)
Sparse Core Ops, SparseCore 0:
  10.2 46.6 all-gather.3
  59.1 52.0 all-gather.5
  113.4 82.8 all-gather.7
  205.4 49.7 reduce-scatter.1
